TPU v7x, 32 devices: a whole 2x2x4 slice. The times are simulated.
32 devices in a mesh: tm: 16 (over z, y, x), col: 2 (over core).
Axes of the slice: x: 2, y: 2, z: 4, core: 2. Of those that a mesh axis runs over, the one named last changes fastest.
Arguments:
- rhs: float32 [16, 1024, 256], P('tm', 'col'), may hold values from -6 to 6
- inverse_blocks: float32 [3, 16, 1024, 1024], P(None, 'tm', None, 'col'), may hold values from -2 to 3, as said below
- lower_coupling: float32 [3, 16, 1024, 1024], P(None, 'tm', None, 'col'), may hold values from -0.1875 to 0.1875
- upper_coupling: float32 [3, 16, 1024, 1024], P(None, 'tm', None, 'col'), may hold values from -0.1875 to 0.1875
- tile_pattern: int32 [3, 16, 2, 8, 8], P(None, 'tm', None, None, 'col'), may hold values from 0 to 1, as said below
- tip_coupling: float32 [3, 16, 64, 1024], P(None, 'tm', None, 'col'), may hold values from -0.046875 to 0.046875
- tip_rhs: float32 [64, 256], replicated, may hold values from -6 to 6
Outputs:
- reduced: float32 [16, 1024, 256], P('tm', 'col')
- tip_reduced: float32 [64, 256], replicated
Inputs may be any that keep to these rules, and one draw needn't show every extreme that they name: Every inverse_blocks[l, j] is symmetric. tile_pattern[l, j, k, r, c] is 1 exactly where |r - c| is at most a half-width w[l, j, k] of 1 to 4; both half-widths 1 and 4 occur.
All inputs are finite; a program needn't handle non-finite values.
Results may differ from a plain program's by a relative error of at most 0.0001.
Values sent between devices are 32-bit elements; how exact they have to be, the bound alone decides.
A program may use at most 64 MiB of HBM per device.

v0:
```python
import functools

import jax
import jax.numpy as jnp
from jax import lax
from jax.experimental import pallas as pl
from jax.experimental.pallas import tpu as pltpu
from jax.sharding import PartitionSpec as P

MESH = pl.DeviceIdType.MESH
LANES = 128
ROWS = 8


def halves_of(x):
    high = x.astype(jnp.bfloat16)
    low = (x - high.astype(jnp.float32)).astype(jnp.bfloat16)
    return high, low


def product(stacked, high, w_high, w_low):
    rows = high.shape[0]
    both = jnp.dot(stacked, w_high, preferred_element_type=jnp.float32)
    return both[:rows] + both[rows:] + jnp.dot(high, w_low, preferred_element_type=jnp.float32)


def kernel(
    dims,
    rhs_hbm,
    inv_hbm,
    low_hbm,
    up_hbm,
    pattern,
    tip_c,
    tip_rhs,
    out,
    tip_out,
    rhs_v,
    raw,
    w_high,
    w_low,
    cur,
    sol,
    send,
    recv,
    joined,
    tip_acc,
    tip_in,
    tip_sum,
    tip_all,
    in_sem,
    rhs_sem,
    cur_s,
    cur_r,
    sol_s,
    sol_r,
    row_s,
    row_r,
    tip_s1,
    tip_r1,
    tip_s2,
    tip_r2,
):
    levels, T, C, block, m, R, F, tiles_all, H = dims
    tiles_here = m * tiles_all // block
    tile = block // tiles_all
    part = R // H
    N = T * C
    row = lax.axis_index("tm")
    col = lax.axis_index("col")
    me = row * C + col
    groups = F // ROWS
    blocks = part // LANES
    G = groups * blocks * H

    sources = (inv_hbm, low_hbm, up_hbm)

    def load(level, kind):
        return pltpu.make_async_copy(
            sources[kind].at[level, 0], raw.at[level, kind], in_sem.at[level, kind]
        )

    rhs_copy = pltpu.make_async_copy(rhs_hbm.at[0], rhs_v, rhs_sem)
    rhs_copy.start()
    for level in range(levels):
        for kind in range(3):
            load(level, kind).start()

    barrier = pltpu.get_barrier_semaphore()

    @pl.loop(1, N)
    def _(k):
        other = lax.rem(me + k, N)
        pl.semaphore_signal(
            barrier,
            inc=1,
            device_id={"tm": other // C, "col": lax.rem(other, C)},
            device_id_type=MESH,
        )

    rhs_copy.wait()
    cur[0, col] = rhs_v[...].T

    def split(level, kind):
        load(level, kind).wait()

        @pl.loop(0, tiles_all)
        def _(r):
            rows = pl.ds(pl.multiple_of(r * tile, tile), tile)
            for c in range(tiles_here):
                cols = pl.ds(c * tile, tile)
                w = raw[level, kind, rows, cols]
                if kind:
                    at = ((level * 2 + kind - 1) * tiles_all + r) * tiles_here + c
                    w = w * pattern[at]
                high, low = halves_of(w)
                w_high[level, kind, rows, cols] = high
                w_low[level, kind, rows, cols] = low

    def rows_of(h):
        return pl.ds(h * part, part)

    def col_copy(buf, sems_s, sems_r, level, h, k, owner, target):
        return pltpu.make_async_remote_copy(
            src_ref=buf.at[level, owner, rows_of(h)],
            dst_ref=buf.at[level, owner, rows_of(h)],
            send_sem=sems_s.at[level, h, k - 1],
            recv_sem=sems_r.at[level, h, k - 1],
            device_id={"tm": row, "col": target},
            device_id_type=MESH,
        )

    def share(buf, sems_s, sems_r, level, h):
        for k in range(1, C):
            col_copy(buf, sems_s, sems_r, level, h, k, col, lax.rem(col + k, C)).start()

    def arrived(buf, sems_s, sems_r, level, h, k):
        owner = lax.rem(col + C - k, C)
        col_copy(buf, sems_s, sems_r, level, h, k, owner, owner).wait_recv()

    def bit_of(level):
        return lax.rem(row // 2**level, 2)

    def row_copy(level, h, way):
        stride = 2**level
        if level == levels - 1:
            target = lax.rem(row + (T - stride if way == 0 else stride), T)
            source = send.at[level, way, rows_of(h)]
        elif way == 0:
            target = lax.rem(row + T - 2 * stride + 4 * stride * bit_of(level), T)
            source = send.at[level, bit_of(level), rows_of(h)]
        else:
            target = row + stride - 2 * stride * bit_of(level)
            source = joined.at[level, rows_of(h)]
        return pltpu.make_async_remote_copy(
            src_ref=source,
            dst_ref=recv.at[level, way, rows_of(h)],
            send_sem=row_s.at[level, h, way],
            recv_sem=row_r.at[level, h, way],
            device_id={"tm": target, "col": col},
            device_id_type=MESH,
        )

    def join(level, h):
        row_copy(level, h, 0).wait_recv()
        joined[level, rows_of(h)] = (
            send[level, 1 - bit_of(level), rows_of(h)] + recv[level, 0, rows_of(h)]
        )
        row_copy(level, h, 1).start()

    def term(buf, level, h, k, kinds, totals):
        owner = lax.rem(col + C - k, C)
        high, low = halves_of(buf[level, owner, rows_of(h)])
        stacked = jnp.concatenate([high, low], axis=0)
        rows = pl.ds(pl.multiple_of(owner * m, m), m)
        results = []
        for kind, total in zip(kinds, totals):
            value = product(stacked, high, w_high[level, kind, rows], w_low[level, kind, rows])
            results.append(value if total is None else total + value)
        return results

    def owner_of(t):
        return (t * N) // G

    def tip_copy1(t):
        owner = owner_of(t)
        slot = lax.rem(me - owner + N, N) - 1
        return pltpu.make_async_remote_copy(
            src_ref=tip_acc.at[t],
            dst_ref=tip_in.at[slot],
            send_sem=tip_s1.at[t],
            recv_sem=tip_r1,
            device_id={"tm": owner // C, "col": lax.rem(owner, C)},
            device_id_type=MESH,
        )

    def tip_copy2(k, t):
        other = lax.rem(me + k, N)
        return pltpu.make_async_remote_copy(
            src_ref=tip_sum,
            dst_ref=tip_all.at[t],
            send_sem=tip_s2.at[k - 1],
            recv_sem=tip_r2.at[t],
            device_id={"tm": other // C, "col": lax.rem(other, C)},
            device_id_type=MESH,
        )

    def each_tile(action):
        @pl.loop(0, G)
        def _(t):
            @pl.when(owner_of(t) != me)
            def _():
                action(t)

    def each_owned(action):
        @pl.loop(0, G)
        def _(t):
            @pl.when(owner_of(t) == me)
            def _():
                action(t)

    def each_other(action):
        @pl.loop(1, N)
        def _(k):
            action(k)

    def add_tip(level, h):
        high, low = halves_of(sol[level, col, rows_of(h)])
        t_high, t_low = halves_of(tip_c[level, 0])
        nt = (((1,), (1,)), ((), ()))
        dot = functools.partial(lax.dot_general, preferred_element_type=jnp.float32)
        value = dot(t_high, high, nt) + dot(t_high, low, nt) + dot(t_low, high, nt)
        for b in range(blocks):
            piece = value[:, b * LANES : (b + 1) * LANES].reshape(groups, ROWS, LANES)
            at = pl.ds((h * blocks + b) * groups, groups)
            if level == 0:
                tip_acc[at] = piece
            else:
                tip_acc[at] = tip_acc[at] + piece

    def settled(level, h):
        row_copy(level, h, 1).wait_recv()
        value = cur[level, col, rows_of(h)] - recv[level, 1, rows_of(h)]
        if level == levels - 1:
            row_copy(level, h, 0).wait_recv()
            value = value - recv[level, 0, rows_of(h)]
        return value

    for kind in range(3):
        split(0, kind)
    pl.semaphore_wait(barrier, N - 1)
    for h in range(H):
        share(cur, cur_s, cur_r, 0, h)

    for level in range(levels):
        for h in range(H):
            if level:
                cur[level, col, rows_of(h)] = settled(level - 1, h)
                share(cur, cur_s, cur_r, level, h)
            total = [None]
            for k in range(C):
                if k:
                    arrived(cur, cur_s, cur_r, level, h, k)
                total = term(cur, level, h, k, (0,), total)
            sol[level, col, rows_of(h)] = total[0]
            share(sol, sol_s, sol_r, level, h)
            add_tip(level, h)
            if level == levels - 1 and h == H - 1:
                each_tile(lambda t: tip_copy1(t).start())
            if level < levels - 1:
                ways = (bit_of(level), 1 - bit_of(level))
            else:
                ways = (0, 1)
            kinds = (1 + ways[0], 1 + ways[1])
            totals = [None, None]
            for k in range(C - 1):
                if k:
                    arrived(sol, sol_s, sol_r, level, h, k)
                totals = term(sol, level, h, k, kinds, totals)
            k = C - 1
            if k:
                arrived(sol, sol_s, sol_r, level, h, k)
            for i in range(2):
                value = term(sol, level, h, k, kinds[i : i + 1], totals[i : i + 1])[0]
                send[level, ways[i], rows_of(h)] = value
                if i == 0 or level == levels - 1:
                    row_copy(level, h, i).start()
        if level < levels - 1:
            for h in range(H):
                join(level, h)
            for kind in range(3):
                split(level + 1, kind)

    def reduce_mine(t):
        pltpu.make_async_copy(tip_in, tip_in, tip_r1).wait()
        tip_sum[...] = tip_acc[t] + jnp.sum(tip_in[...], axis=0)
        tip_all[t] = tip_sum[...]
        each_other(lambda k: tip_copy2(k, t).start())

    each_owned(reduce_mine)
    for h in range(H):
        out[0, :, h * part : (h + 1) * part] = settled(levels - 1, h).T
    each_tile(lambda t: tip_copy2(1, t).wait_recv())
    for h in range(H):
        for b in range(blocks):
            at = h * blocks + b
            lanes = slice(at * LANES, (at + 1) * LANES)
            total = tip_all[at * groups : (at + 1) * groups].reshape(F, LANES)
            tip_out[:, lanes] = tip_rhs[:, lanes] - total

    for level in range(levels):
        for h in range(H):
            for k in range(1, C):
                target = lax.rem(col + k, C)
                col_copy(cur, cur_s, cur_r, level, h, k, col, target).wait_send()
                col_copy(sol, sol_s, sol_r, level, h, k, col, target).wait_send()
            for way in range(2):
                row_copy(level, h, way).wait_send()
    each_tile(lambda t: tip_copy1(t).wait_send())
    each_owned(lambda t: each_other(lambda k: tip_copy2(k, t).wait_send()))


HALVES = 2


def solution(mesh):
    T, C = mesh.shape["tm"], mesh.shape["col"]

    def local(rhs, inverse, lower, upper, tile_pattern, tip_coupling, tip_rhs):
        levels, _, block, m = inverse.shape
        R = rhs.shape[2]
        F = tip_rhs.shape[0]
        H = HALVES
        dims = (levels, T, C, block, m, R, F, tile_pattern.shape[3], H)
        N = T * C
        G = (F // ROWS) * (R // LANES)
        f32, b16 = jnp.float32, jnp.bfloat16
        dma = pltpu.SemaphoreType.DMA
        peers = max(C - 1, 1)
        anywhere = pl.BlockSpec(memory_space=pl.ANY)
        vmem = pl.BlockSpec(memory_space=pltpu.VMEM)
        return pl.pallas_call(
            functools.partial(kernel, dims),
            out_shape=(
                jax.ShapeDtypeStruct((1, m, R), f32),
                jax.ShapeDtypeStruct((F, R), f32),
            ),
            in_specs=[anywhere] * 4 + [pl.BlockSpec(memory_space=pltpu.SMEM), vmem, vmem],
            out_specs=(vmem, vmem),
            scratch_shapes=[
                pltpu.VMEM((m, R), f32),
                pltpu.VMEM((levels, 3, block, m), f32),
                pltpu.VMEM((levels, 3, block, m), b16),
                pltpu.VMEM((levels, 3, block, m), b16),
                pltpu.VMEM((levels, C, R, m), f32),
                pltpu.VMEM((levels, C, R, m), f32),
                pltpu.VMEM((levels, 2, R, m), f32),
                pltpu.VMEM((levels, 2, R, m), f32),
                pltpu.VMEM((max(levels - 1, 1), R, m), f32),
                pltpu.VMEM((G, ROWS, LANES), f32),
                pltpu.VMEM((N - 1, ROWS, LANES), f32),
                pltpu.VMEM((ROWS, LANES), f32),
                pltpu.VMEM((G, ROWS, LANES), f32),
                dma((levels, 3)),
                dma,
                dma((levels, H, peers)),
                dma((levels, H, peers)),
                dma((levels, H, peers)),
                dma((levels, H, peers)),
                dma((levels, H, 2)),
                dma((levels, H, 2)),
                dma((G,)),
                dma,
                dma((N - 1,)),
                dma((G,)),
            ],
            compiler_params=pltpu.CompilerParams(
                collective_id=0, has_side_effects=True, vmem_limit_bytes=60 * 2**20
            ),
        )(
            rhs,
            inverse,
            lower,
            upper,
            tile_pattern.astype(f32).reshape(-1),
            tip_coupling,
            tip_rhs,
        )

    return jax.shard_map(
        local,
        mesh=mesh,
        in_specs=(
            P("tm", "col", None),
            P(None, "tm", None, "col"),
            P(None, "tm", None, "col"),
            P(None, "tm", None, "col"),
            P(None, "tm", None, None, "col"),
            P(None, "tm", None, "col"),
            P(),
        ),
        out_specs=(P("tm", "col", None), P()),
        check_vma=False,
    )
```

profile of v0, /device:TPU:0, one launch (start us, length us, event | category | flops | bytes accessed | tf_op | source)
XLA Modules:
  0.0 88.7 jit_solution(15461999242870809117)
XLA Ops:
  0.6 0.7 convert_element_type.3
  1.3 0.1 copy.9
  1.5 0.7 reshape.7.pattern
  2.1 83.3 %shard_map.86 = (f32[1,512,256]{2,1,0:T(8,128)}, f32[64,256]{1,0:T(8,128)}) custom-call(f32[1,512,256]{2,1,0:T(8,128)} %rhs_hbm.1, f32[3,1,1024,512]{3,2,1,0:T(8,128)} %inv_hbm.1, f32[3,1,1024,512]{3,2,1,0:T(8,128)} %low_hbm.1, f32[3,1,1024,512]{3,2,1,0:T(8,128)} %up_hbm.1, f32[192]{0:T(256)} %reshape.7.pattern, f32[3,1,64,512]{3,2,1,0:T(8,128)} %tip_c.1, ...), custom_call_target="tpu_custom_call" | custom-call | tf_op jit(solution)/shard_map/pallas_call | solution.py:342
  85.4 1.9 %copy.12 = f32[1,512,256]{2,1,0:T(8,128)} copy(f32[1,512,256]{2,1,0:T(8,128)} %get-tuple-element.4) | data formatting | bytes 1048576
  87.3 1.5 %copy.13 = f32[64,256]{1,0:T(8,128)} copy(f32[64,256]{1,0:T(8,128)} %get-tuple-element.5) | data formatting | bytes 131072
where the time goes:
time: 89 us; the launch traced here: 88.7 us
  Pallas kernels  83.3 us (94%)
  local copies, waits for them, and re-layouts  4.12 us (5%)
    pallas_call x1, Pallas kernels, local(): pl.pallas_call(functools.partial(kernel, dims), out_shape=(jax.ShapeDtype...  83.3 us
    unnamed x2, local copies, waits for them, and re-layouts  3.34 us

commit v1 on v0

v1 whole, which is shorter than its diff:
```python
import contextlib
import functools

import jax
import jax.numpy as jnp
from jax import lax
from jax.experimental import pallas as pl
from jax.experimental.pallas import tpu as pltpu
from jax.sharding import PartitionSpec as P

MESH = pl.DeviceIdType.MESH
LANES = 128
ROWS = 8
TRACE = False
NT = (((1,), (1,)), ((), ()))
NN = (((1,), (0,)), ((), ()))


def scope(name):
    return jax.named_scope(name) if TRACE else contextlib.nullcontext()


def halves_of(x):
    high = x.astype(jnp.bfloat16)
    low = (x - high.astype(jnp.float32)).astype(jnp.bfloat16)
    return high, low


def product(stacked, high, w_high, w_low, form):
    rows = high.shape[0]
    dot = functools.partial(
        lax.dot_general, dimension_numbers=form, preferred_element_type=jnp.float32
    )
    both = dot(stacked, w_high)
    return both[:rows] + both[rows:] + dot(high, w_low)


ORDER = (
    "S00", "P01", "P02", "S01", "P03", "J00", "S02", "K00", "W20", "W12", "W11", "J01",
    "S03", "K01", "W10", "P10", "J02", "K02", "S10", "J03", "P11", "K03", "P12", "J10",
    "S11", "K10", "S12", "P13", "W21", "W22", "J11", "S13", "P20", "K11", "J12", "S20",
    "K12", "J13", "P21", "K13", "S21", "P22", "P23", "S22", "S23",
)
PIECES = 4


def pieces(R):
    return tuple((R * h // PIECES, R // PIECES) for h in range(PIECES))


def kernel(
    dims,
    rhs_hbm,
    inv_hbm,
    low_hbm,
    up_hbm,
    pattern,
    tip_c_hbm,
    tip_rhs_hbm,
    out,
    tip_out,
    rhs_v,
    tip_c,
    tip_rhs,
    raw,
    w_high,
    w_low,
    cur,
    part,
    stk,
    send,
    recv,
    joined,
    tip_acc,
    tip_near,
    tip_far,
    tip_all,
    in_sem,
    rhs_sem,
    part_s,
    part_r,
    row_s,
    row_r,
    near_s,
    near_r,
    far_s,
    far_r,
    gather_s,
    gather_r,
):
    levels, T, C, block, m, R, F, tiles_all, bits, cuts = dims
    tiles_here = m * tiles_all // block
    tile = block // tiles_all
    N = T * C
    row = lax.axis_index("tm")
    col = lax.axis_index("col")
    me = row * C + col
    groups = F // ROWS
    G = groups * (R // LANES)
    parts = pieces(R)
    H = len(parts)
    last = levels - 1

    sources = (inv_hbm, low_hbm, up_hbm)

    def load(level, kind):
        return pltpu.make_async_copy(
            sources[kind].at[level, 0], raw.at[level, kind], in_sem.at[level, kind]
        )

    rhs_copy = pltpu.make_async_copy(rhs_hbm.at[0], rhs_v, rhs_sem.at[0])
    tip_c_copy = pltpu.make_async_copy(tip_c_hbm, tip_c, rhs_sem.at[1])
    tip_rhs_copy = pltpu.make_async_copy(tip_rhs_hbm, tip_rhs, rhs_sem.at[2])
    rhs_copy.start()
    load(0, 0).start()

    barrier = pltpu.get_barrier_semaphore()

    def greet(device):
        pl.semaphore_signal(barrier, inc=1, device_id=device, device_id_type=MESH)

    near = 2**bits * C
    each = G // near
    Q = T // 2**bits
    place = row // 2**bits
    seat = lax.rem(row, 2**bits) * C + col

    def over(count, action):
        @pl.loop(1, count)
        def _(k):
            action(k)

    def near_of(k):
        other = lax.rem(seat + k, near)
        return other, {"tm": place * 2**bits + other // C, "col": lax.rem(other, C)}

    def far_of(k):
        other = lax.rem(place + k, Q)
        return {"tm": other * 2**bits + lax.rem(row, 2**bits), "col": col}

    by_fours = bits == 2 and levels == 3

    def announce():
        if not by_fours:

            def anyone(k):
                other = lax.rem(me + k, N)
                greet({"tm": other // C, "col": lax.rem(other, C)})

            return over(N, anyone)
        over(near, lambda k: greet(near_of(k)[1]))
        over(Q, lambda k: greet(far_of(k)))
        inner = bit_of(0) != bit_of(1)

        @pl.when(inner)
        def _():
            beyond = lax.rem(row + 2 + (T - 4) * bit_of(0), T)
            greet({"tm": beyond, "col": col})

    def met():
        if not by_fours:
            return pl.semaphore_wait(barrier, N - 1)
        outer = 1 - lax.rem(bit_of(0) + bit_of(1), 2)
        pl.semaphore_wait(barrier, near - 1 + Q - 1 + outer)

    def bit_of(level):
        return lax.rem(row // 2**level, 2)

    announce()

    def split(level, kind):
        load(level, kind).wait()

        @pl.loop(0, tiles_all)
        def _(r):
            rows = pl.ds(pl.multiple_of(r * tile, tile), tile)
            for c in range(tiles_here):
                cols = pl.ds(c * tile, tile)
                w = raw[level, kind, rows, cols]
                if kind:
                    w = w * pattern[level, 0, kind - 1, c, r].astype(jnp.float32)
                high, low = halves_of(w)
                w_high[level, kind, rows, cols] = high
                w_low[level, kind, rows, cols] = low

    def rows_of(h):
        return pl.ds(parts[h][0], parts[h][1])

    def part_copy(level, h, k):
        return pltpu.make_async_remote_copy(
            src_ref=part.at[level, 0, rows_of(h)],
            dst_ref=part.at[level, k, rows_of(h)],
            send_sem=part_s.at[level, h, k - 1],
            recv_sem=part_r.at[level, h, k - 1],
            device_id={"tm": row, "col": lax.rem(col + k, C)},
            device_id_type=MESH,
        )

    def cuts_of(level):
        return 1 if level == last else cuts

    def span(level, q):
        width = m // cuts_of(level)
        return pl.ds(q * width, width)

    def row_copy(level, h, way, q):
        stride = 2**level
        at = (rows_of(h), span(level, q))
        if level == last:
            target = lax.rem(row + (T - stride if way == 0 else stride), T)
            source = send.at[(level, way, *at)]
        elif way == 0:
            target = lax.rem(row + T - 2 * stride + 4 * stride * bit_of(level), T)
            source = send.at[(level, bit_of(level), *at)]
        else:
            target = row + stride - 2 * stride * bit_of(level)
            source = joined.at[(level, *at)]
        return pltpu.make_async_remote_copy(
            src_ref=source,
            dst_ref=recv.at[(level, way, *at)],
            send_sem=row_s.at[level, h, way, q],
            recv_sem=row_r.at[level, h, way, q],
            device_id={"tm": target, "col": col},
            device_id_type=MESH,
        )

    def join(level, h, q):
        row_copy(level, h, 0, q).wait_recv()
        at = (rows_of(h), span(level, q))
        joined[(level, *at)] = (
            send[(level, 1 - bit_of(level), *at)] + recv[(level, 0, *at)]
        )
        row_copy(level, h, 1, q).start()

    def settled(level, h):
        for q in range(cuts_of(level)):
            row_copy(level, h, 1, q).wait_recv()
        value = cur[level, rows_of(h)] - recv[level, 1, rows_of(h)]
        if level == last:
            row_copy(level, h, 0, 0).wait_recv()
            value = value - recv[level, 0, rows_of(h)]
        return value

    def solve(level, h):
        if level:
            with scope(f"settle{level}{h}"):
                cur[level, rows_of(h)] = settled(level - 1, h)
        with scope(f"P{level}{h}"):
            high, low = halves_of(cur[level, rows_of(h)])
            stacked = jnp.concatenate([high, low], axis=0)
            part[level, 0, rows_of(h)] = product(
                stacked, high, w_high[level, 0], w_low[level, 0], NT
            )
            for k in range(1, C):
                part_copy(level, h, k).start()

    def add_tip(level, h, n):
        mine = pl.ds(pl.multiple_of(col * m, m), m)
        high, low = stk[0:n, mine], stk[n : 2 * n, mine]
        t_high, t_low = halves_of(tip_c[level, 0])
        dot = functools.partial(
            lax.dot_general, dimension_numbers=NT, preferred_element_type=jnp.float32
        )
        value = dot(t_high, high) + dot(t_high, low) + dot(t_low, high)
        start = parts[h][0]
        done = 0
        while done < n:
            b, lane = (start + done) // LANES, (start + done) % LANES
            w = min(LANES - lane, n - done)
            piece = value[:, done : done + w].reshape(groups, ROWS, w)
            at = (pl.ds(b * groups, groups), slice(None), pl.ds(lane, w))
            if level == 0:
                tip_acc[at] = piece
            else:
                tip_acc[at] = tip_acc[at] + piece
            done += w

    def spread(level, h):
        n = parts[h][1]
        with scope(f"xwait{level}{h}"):
            for k in range(1, C):
                part_copy(level, h, k).wait_recv()
        with scope(f"S{level}{h}"):
            total = part[level, 0, rows_of(h)]
            for k in range(1, C):
                total = total + part[level, k, rows_of(h)]
            high, low = halves_of(total)
            stk[0:n] = high
            stk[n : 2 * n] = low
        if level < last:
            ways = (bit_of(level), 1 - bit_of(level))
        else:
            ways = (0, 1)
        if level == last:
            with scope(f"tip{level}{h}"):
                add_tip(level, h, n)
                if h == H - 1:
                    tip_scatter()
        for i in range(2):
            for q in range(cuts_of(level)):
                with scope(f"DU{level}{h}"):
                    at = span(level, q)
                    send[level, ways[i], rows_of(h), at] = product(
                        stk[0 : 2 * n],
                        stk[0:n],
                        w_high[level, 1 + ways[i], :, at],
                        w_low[level, 1 + ways[i], :, at],
                        NN,
                    )
                    if level == last and h == H - 1:
                        continue
                    if i == 0 or level == last:
                        row_copy(level, h, i, q).start()
        if level < last:
            with scope(f"tip{level}{h}"):
                add_tip(level, h, n)

    def scatter_copy(k):
        other, device = near_of(k)
        return pltpu.make_async_remote_copy(
            src_ref=tip_acc.at[pl.ds(other * each, each)],
            dst_ref=tip_near.at[k - 1],
            send_sem=near_s.at[k - 1],
            recv_sem=near_r.at[k - 1],
            device_id=device,
            device_id_type=MESH,
        )

    def far_copy(k, here=True):
        slot = place if here else lax.rem(place + Q - k, Q)
        return pltpu.make_async_remote_copy(
            src_ref=tip_far.at[slot],
            dst_ref=tip_far.at[slot],
            send_sem=far_s.at[k - 1],
            recv_sem=far_r.at[k - 1],
            device_id=far_of(k),
            device_id_type=MESH,
        )

    def gather_copy(k, here=True):
        slot = seat if here else lax.rem(seat + near - k, near)
        return pltpu.make_async_remote_copy(
            src_ref=tip_all.at[pl.ds(slot * each, each)],
            dst_ref=tip_all.at[pl.ds(slot * each, each)],
            send_sem=gather_s.at[k - 1],
            recv_sem=gather_r.at[k - 1],
            device_id=near_of(k)[1],
            device_id_type=MESH,
        )

    def tip_scatter():
        over(near, lambda k: scatter_copy(k).start())

    def tip_reduce():
        over(near, lambda k: scatter_copy(k).wait_recv())
        tip_far[place] = tip_acc[pl.ds(seat * each, each)] + jnp.sum(
            tip_near[...], axis=0
        )
        over(Q, lambda k: far_copy(k).start())

    def tip_total():
        over(Q, lambda k: far_copy(k, False).wait_recv())
        tip_all[pl.ds(seat * each, each)] = jnp.sum(tip_far[...], axis=0)
        over(near, lambda k: gather_copy(k).start())

    def tip_finish():
        over(near, lambda k: gather_copy(k, False).wait_recv())
        tip_rhs_copy.wait()
        for b in range(R // LANES):
            lanes = slice(b * LANES, (b + 1) * LANES)
            total = tip_all[b * groups : (b + 1) * groups].reshape(F, LANES)
            tip_out[:, lanes] = tip_rhs[:, lanes] - total

    def final(h):
        start, n = parts[h]
        out[0, :, start : start + n] = settled(last, h).T

    with scope("rhs"):
        rhs_copy.wait()
        for kind in (1, 2):
            load(0, kind).start()
        cur[0] = rhs_v[...].T
    with scope("split00"):
        split(0, 0)
    tip_c_copy.start()
    tip_rhs_copy.start()
    with scope("barrier"):
        met()
    solve(0, 0)
    for kind in (1, 2):
        with scope("split0"):
            split(0, kind)
    for level in range(1, levels):
        for kind in range(3):
            load(level, kind).start()
    tip_c_copy.wait()

    def splits(level, *kinds):
        for kind in kinds:
            with scope(f"split{level}{kind}"):
                split(level, kind)

    def joins(q, level, h):
        if q < cuts_of(level):
            with scope(f"join{level}{h}"):
                join(level, h, q)

    def finals(h):
        with scope(f"final{h}"):
            final(h)

    actions = {
        "P": solve,
        "S": spread,
        "J": functools.partial(joins, 0),
        "K": functools.partial(joins, 1),
        "W": splits,
    }
    for step in ORDER:
        actions[step[0]](int(step[1]), int(step[2]))
    with scope("tipreduce"):
        tip_reduce()
    for i in range(2):
        row_copy(last, H - 1, i, 0).start()
    for h in range(H - 2):
        finals(h)
    with scope("tiptotal"):
        tip_total()
    finals(H - 2)
    with scope("tipfinish"):
        tip_finish()
    finals(H - 1)

    with scope("drain"):
        for level in range(levels):
            for h in range(H):
                for k in range(1, C):
                    part_copy(level, h, k).wait_send()
                for way in range(2):
                    for q in range(cuts_of(level)):
                        row_copy(level, h, way, q).wait_send()
        over(near, lambda k: scatter_copy(k).wait_send())
        over(Q, lambda k: far_copy(k).wait_send())
        over(near, lambda k: gather_copy(k).wait_send())


def solution(mesh):
    T, C = mesh.shape["tm"], mesh.shape["col"]

    def local(rhs, inverse, lower, upper, tile_pattern, tip_coupling, tip_rhs):
        levels, _, block, m = inverse.shape
        R = rhs.shape[2]
        F = tip_rhs.shape[0]
        G = (F // ROWS) * (R // LANES)
        cuts = 2 if m % (2 * LANES) == 0 else 1
        bits = 0
        while bits < 2 and G % (2 ** (bits + 1) * C) == 0 and T % 2 ** (bits + 1) == 0:
            bits += 1
        dims = (levels, T, C, block, m, R, F, tile_pattern.shape[3], bits, cuts)
        H = len(pieces(R))
        widest = max(n for _, n in pieces(R))
        Q = T // 2**bits
        f32, b16 = jnp.float32, jnp.bfloat16
        dma = pltpu.SemaphoreType.DMA
        peers = max(C - 1, 1)
        near = 2**bits * C
        anywhere = pl.BlockSpec(memory_space=pl.ANY)
        vmem = pl.BlockSpec(memory_space=pltpu.VMEM)
        return pl.pallas_call(
            functools.partial(kernel, dims),
            out_shape=(
                pltpu.VMEM((1, m, R), f32),
                pltpu.VMEM((F, R), f32),
            ),
            in_specs=[anywhere] * 4
            + [pl.BlockSpec(memory_space=pltpu.SMEM), anywhere, anywhere],
            out_specs=(vmem, vmem),
            scratch_shapes=[
                pltpu.VMEM((m, R), f32),
                pltpu.VMEM((levels, 1, F, m), f32),
                pltpu.VMEM((F, R), f32),
                pltpu.VMEM((levels, 3, block, m), f32),
                pltpu.VMEM((levels, 3, block, m), b16),
                pltpu.VMEM((levels, 3, block, m), b16),
                pltpu.VMEM((levels, R, m), f32),
                pltpu.VMEM((levels, C, R, block), f32),
                pltpu.VMEM((2 * widest, block), b16),
                pltpu.VMEM((levels, 2, R, m), f32),
                pltpu.VMEM((levels, 2, R, m), f32),
                pltpu.VMEM((max(levels - 1, 1), R, m), f32),
                pltpu.VMEM((G, ROWS, LANES), f32),
                pltpu.VMEM((near - 1, G // near, ROWS, LANES), f32),
                pltpu.VMEM((Q, G // near, ROWS, LANES), f32),
                pltpu.VMEM((G, ROWS, LANES), f32),
                dma((levels, 3)),
                dma((3,)),
                dma((levels, H, peers)),
                dma((levels, H, peers)),
                dma((levels, H, 2, cuts)),
                dma((levels, H, 2, cuts)),
                dma((near - 1,)),
                dma((near - 1,)),
                dma((Q - 1,)),
                dma((Q - 1,)),
                dma((near - 1,)),
                dma((near - 1,)),
            ],
            compiler_params=pltpu.CompilerParams(
                collective_id=0, has_side_effects=True, vmem_limit_bytes=63 * 2**20
            ),
        )(
            rhs,
            inverse,
            lower,
            upper,
            jnp.swapaxes(tile_pattern, 3, 4),
            tip_coupling,
            tip_rhs,
        )

    return jax.shard_map(
        local,
        mesh=mesh,
        in_specs=(
            P("tm", "col", None),
            P(None, "tm", None, "col"),
            P(None, "tm", None, "col"),
            P(None, "tm", None, "col"),
            P(None, "tm", None, None, "col"),
            P(None, "tm", None, "col"),
            P(),
        ),
        out_specs=(P("tm", "col", None), P()),
        check_vma=False,
    )
```

time: 89 us -> 65.7 us (0.74)
  Pallas kernels: 83.3 us -> 63.4 us
  local copies, waits for them, and re-layouts: 4.12 us -> 1.42 us
    pallas_call x1, Pallas kernels: 83.3 us -> 63.4 us  [local(): pl.pallas_call(functools.partial(kernel, dims), out_shape=(pltpu.VMEM((1,...]
    unnamed x2, local copies, waits for them, and re-layouts: 3.34 us -> 1.42 us
where the time goes in v1:
time: 65.7 us; the launch traced here: 65.5 us
  Pallas kernels  63.4 us (96%)
  local copies, waits for them, and re-layouts  1.42 us (2%)
    pallas_call x1, Pallas kernels, local(): pl.pallas_call(functools.partial(kernel, dims), out_shape=(pltpu.VMEM((1,...  63.4 us
    unnamed x2, local copies, waits for them, and re-layouts  1.42 us

profile of v1, /device:TPU:0, one launch (start us, length us, event | category | flops | bytes accessed | tf_op | source)
XLA Modules:
  0.0 65.5 jit_solution(3323951123904471150)
XLA Ops:
  0.6 63.4 %shard_map.86 = (f32[1,512,256]{2,1,0:T(8,128)S(1)}, f32[64,256]{1,0:T(8,128)S(1)}) custom-call(f32[1,512,256]{2,1,0:T(8,128)} %rhs_hbm.1, f32[3,1,1024,512]{3,2,1,0:T(8,128)} %inv_hbm.1, f32[3,1,1024,512]{3,2,1,0:T(8,128)} %low_hbm.1, f32[3,1,1024,512]{3,2,1,0:T(8,128)} %up_hbm.1, s32[3,1,2,4,8]{4,3,2,1,0:T(4,128)} %bitcast.1, f32[3,1,64,512]{3,2,1,0:T(8,128)} %tip_c_hbm.1, ...), custom_call_target="tpu_custom_call" | custom-call | tf_op jit(solution)/shard_map/pallas_call | solution.py:469
  64.1 0.8 %copy.11 = f32[1,512,256]{2,1,0:T(8,128)} copy(f32[1,512,256]{2,1,0:T(8,128)S(1)} %get-tuple-element.2) | data formatting | bytes 1048576
  64.9 0.6 copy.12

commit v2 on v1

v2 whole, which is shorter than its diff:
```python
import contextlib
import functools

import jax
import jax.numpy as jnp
from jax import lax
from jax.experimental import pallas as pl
from jax.experimental.pallas import tpu as pltpu
from jax.sharding import PartitionSpec as P

MESH = pl.DeviceIdType.MESH
LANES = 128
ROWS = 8
TRACE = False
NT = (((1,), (1,)), ((), ()))
NN = (((1,), (0,)), ((), ()))


def scope(name):
    return jax.named_scope(name) if TRACE else contextlib.nullcontext()


def halves_of(x):
    high = x.astype(jnp.bfloat16)
    low = (x - high.astype(jnp.float32)).astype(jnp.bfloat16)
    return high, low


def product(stacked, high, w_high, w_low, form):
    rows = high.shape[0]
    dot = functools.partial(
        lax.dot_general, dimension_numbers=form, preferred_element_type=jnp.float32
    )
    both = dot(stacked, w_high)
    return both[:rows] + both[rows:] + dot(high, w_low)


ORDER = (
    "S00", "P01", "W10", "W11", "J00", "S01", "K00", "W12", "W20", "J01", "W21", "W22",
    "K01", "J02", "P10", "K02", "S10", "J03", "P11", "K03", "S11", "P12", "J10", "S12",
    "K10", "P13", "J11", "S13", "P20", "J12", "S20", "P21", "J13", "S21", "T04", "P22",
    "S22", "T14", "P23", "T23", "S23",
)
PIECES = 4
QUARTERS = 4
PAIRED = (0,)
DIRECT = ()
HALVED = ((0, 0), (0, 1), (0, 2), (0, 3), (1, 0))


def pieces(R):
    return tuple((R * h // PIECES, R // PIECES) for h in range(PIECES))


def kernel(
    dims,
    rhs_hbm,
    inv_hbm,
    low_hbm,
    up_hbm,
    pattern_hbm,
    tip_c_hbm,
    tip_rhs_hbm,
    out,
    tip_out,
    pattern,
    rhs_v,
    tip_c,
    tip_rhs,
    raw,
    w_high,
    w_low,
    cur,
    part,
    s_high,
    s_low,
    send,
    recv,
    joined,
    tip_acc,
    tip_near,
    tip_far,
    tip_all,
    in_sem,
    rhs_sem,
    first_sem,
    part_r,
    join_r,
    row_r,
    tip_r,
    sent,
):
    levels, T, C, block, m, R, F, tiles_all, bits, cuts = dims
    tiles_here = m * tiles_all // block
    tile = block // tiles_all
    N = T * C
    row = lax.axis_index("tm")
    col = lax.axis_index("col")
    me = row * C + col
    groups = F // ROWS
    G = groups * (R // LANES)
    parts = pieces(R)
    H = len(parts)
    last = levels - 1

    sources = (inv_hbm, low_hbm, up_hbm)

    def load(level, kind):
        return pltpu.make_async_copy(
            sources[kind].at[level, 0], raw.at[level, kind], in_sem.at[level, kind]
        )

    def first_load(q):
        rows = pl.ds(q * (block // QUARTERS), block // QUARTERS)
        return pltpu.make_async_copy(
            inv_hbm.at[0, 0, rows], raw.at[0, 0, rows], first_sem.at[q]
        )

    rhs_copy = pltpu.make_async_copy(rhs_hbm.at[0], rhs_v, rhs_sem.at[0])
    pattern_copy = pltpu.make_async_copy(pattern_hbm, pattern, rhs_sem.at[3])
    tip_c_copy = pltpu.make_async_copy(tip_c_hbm, tip_c, rhs_sem.at[1])
    tip_rhs_copy = pltpu.make_async_copy(tip_rhs_hbm, tip_rhs, rhs_sem.at[2])
    rhs_copy.start()
    for q in range(QUARTERS):
        first_load(q).start()
    pattern_copy.start()

    barrier = pltpu.get_barrier_semaphore()

    def greet(device):
        pl.semaphore_signal(barrier, inc=1, device_id=device, device_id_type=MESH)

    near = 2**bits * C
    each = G // near
    Q = T // 2**bits
    place = row // 2**bits
    seat = lax.rem(row, 2**bits) * C + col

    def over(count, action):
        @pl.loop(1, count)
        def _(k):
            action(k)

    def near_of(k):
        other = lax.rem(seat + k, near)
        return other, {"tm": place * 2**bits + other // C, "col": lax.rem(other, C)}

    def far_of(k):
        other = lax.rem(place + k, Q)
        return {"tm": other * 2**bits + lax.rem(row, 2**bits), "col": col}

    by_fours = bits == 2 and levels == 3

    def announce():
        if not by_fours:

            def anyone(k):
                other = lax.rem(me + k, N)
                greet({"tm": other // C, "col": lax.rem(other, C)})

            return over(N, anyone)
        over(near, lambda k: greet(near_of(k)[1]))
        over(Q, lambda k: greet(far_of(k)))
        greet({"tm": lax.rem(row + T - 2 + 4 * bit_of(1), T), "col": col})

        @pl.when(bit_of(0) == bit_of(1))
        def _():
            greet({"tm": lax.rem(row + T - 1 + 2 * bit_of(1), T), "col": col})

    def met():
        if not by_fours:
            return pl.semaphore_wait(barrier, N - 1)
        outer = 1 - lax.rem(bit_of(0) + bit_of(1), 2)
        pl.semaphore_wait(barrier, near + Q - 1 + outer)

    def bit_of(level):
        return lax.rem(row // 2**level, 2)

    announce()

    def split(level, kind):
        if level or kind:
            load(level, kind).wait()
            return split_tiles(level, kind, 0, tiles_all)
        for q in range(QUARTERS):
            first_load(q).wait()
            split_tiles(0, 0, tiles_all * q // QUARTERS, tiles_all * (q + 1) // QUARTERS)

    def split_tiles(level, kind, begin, end):
        @pl.loop(begin, end)
        def _(r):
            rows = pl.ds(pl.multiple_of(r * tile, tile), tile)
            for c in range(tiles_here):
                cols = pl.ds(c * tile, tile)
                w = raw[level, kind, rows, cols]
                if kind:
                    w = w * pattern[level, 0, kind - 1, c, r].astype(jnp.float32)
                high, low = halves_of(w)
                w_high[level, kind, rows, cols] = high
                w_low[level, kind, rows, cols] = low

    def all_of(ref, sem):
        pltpu.make_async_copy(ref, ref, sem).wait()

    def rows_of(h):
        return pl.ds(parts[h][0], parts[h][1])

    def group(level, g):
        width = 2 if level in PAIRED else 1
        return range(g * width, (g + 1) * width)

    def groups_of(level):
        return H // 2 if level in PAIRED else H

    def rows_in(level, g):
        members = group(level, g)
        start = parts[members[0]][0]
        return pl.ds(start, parts[members[-1]][0] + parts[members[-1]][1] - start)

    def part_copy(level, g, k):
        return pltpu.make_async_remote_copy(
            src_ref=part.at[level, 0, rows_in(level, g)],
            dst_ref=part.at[level, k, rows_in(level, g)],
            send_sem=sent.at[0],
            recv_sem=part_r.at[level, g, k - 1],
            device_id={"tm": row, "col": lax.rem(col + k, C)},
            device_id_type=MESH,
        )

    def direct(level, h):
        return level == last or (level, h) in DIRECT

    def cuts_of(level, h):
        return cuts if (level, h) in HALVED and not direct(level, h) else 1

    def span(level, h, q):
        width = m // cuts_of(level, h)
        return pl.ds(q * width, width)

    def row_copy(level, h, way, q):
        stride = 2**level
        at = (rows_of(h), span(level, h, q))
        arrival = row_r.at[level, h]
        if direct(level, h):
            target = lax.rem(row + (T - stride if way == 0 else stride), T)
            source = send.at[(level, way, *at)]
        elif way == 0:
            target = lax.rem(row + T - 2 * stride + 4 * stride * bit_of(level), T)
            source = send.at[(level, bit_of(level), *at)]
            arrival = join_r.at[level, h, q]
        else:
            target = row + stride - 2 * stride * bit_of(level)
            source = joined.at[(level, *at)]
        return pltpu.make_async_remote_copy(
            src_ref=source,
            dst_ref=recv.at[(level, way, *at)],
            send_sem=sent.at[1],
            recv_sem=arrival,
            device_id={"tm": target, "col": col},
            device_id_type=MESH,
        )

    def join(level, h, q):
        row_copy(level, h, 0, q).wait_recv()
        at = (rows_of(h), span(level, h, q))
        joined[(level, *at)] = (
            send[(level, 1 - bit_of(level), *at)] + recv[(level, 0, *at)]
        )
        row_copy(level, h, 1, q).start()

    def settled(level, h):
        ways = pl.ds(0, 2) if direct(level, h) else pl.ds(1, 1)
        all_of(recv.at[level, ways, rows_of(h)], row_r.at[level, h])
        value = cur[level, rows_of(h)] - recv[level, 1, rows_of(h)]
        if direct(level, h):
            value = value - recv[level, 0, rows_of(h)]
        return value

    def solve(level, g):
        if level:
            for h in group(level, g):
                with scope(f"settle{level}{h}"):
                    cur[level, rows_of(h)] = settled(level - 1, h)
        with scope(f"P{level}{g}"):
            rows = rows_in(level, g)
            high, low = halves_of(cur[level, rows])
            stacked = jnp.concatenate([high, low], axis=0)
            part[level, 0, rows] = product(
                stacked, high, w_high[level, 0], w_low[level, 0], NT
            )
            for k in range(1, C):
                part_copy(level, g, k).start()

    def add_tip(level, first, end):
        start = parts[first][0]
        n = parts[end - 1][0] + parts[end - 1][1] - start
        mine = pl.ds(pl.multiple_of(col * m, m), m)
        high = s_high[level, pl.ds(start, n), mine]
        low = s_low[level, pl.ds(start, n), mine]
        t_high, t_low = halves_of(tip_c[level, 0])
        dot = functools.partial(
            lax.dot_general, dimension_numbers=NT, preferred_element_type=jnp.float32
        )
        value = dot(t_high, high) + dot(t_high, low) + dot(t_low, high)
        done = 0
        while done < n:
            b, lane = (start + done) // LANES, (start + done) % LANES
            w = min(LANES - lane, n - done)
            piece = value[:, done : done + w].reshape(groups, ROWS, w)
            at = (pl.ds(b * groups, groups), slice(None), pl.ds(lane, w))
            if level == 0:
                tip_acc[at] = piece
            else:
                tip_acc[at] = tip_acc[at] + piece
            done += w

    def spread(level, g):
        rows = rows_in(level, g)
        members = group(level, g)
        closing = level == last and members[-1] == H - 1
        with scope(f"xwait{level}{g}"):
            for k in range(1, C):
                part_copy(level, g, k).wait_recv()
        with scope(f"S{level}{g}"):
            total = part[level, 0, rows]
            for k in range(1, C):
                total = total + part[level, k, rows]
            high, low = halves_of(total)
            s_high[level, rows] = high
            s_low[level, rows] = low
        straight = direct(level, members[0])
        ways = (0, 1) if straight else (bit_of(level), 1 - bit_of(level))
        if closing:
            with scope(f"tip{level}{g}"):
                add_tip(level, members[0], H)
                tip_scatter()
        for i in range(2):
            with scope(f"DU{level}{g}"):
                high = s_high[level, rows]
                stacked = jnp.concatenate([high, s_low[level, rows]], axis=0)
                send[level, ways[i], rows] = product(
                    stacked,
                    high,
                    w_high[level, 1 + ways[i]],
                    w_low[level, 1 + ways[i]],
                    NN,
                )
                if not closing and (i == 0 or straight):
                    for h in members:
                        for q in range(cuts_of(level, h)):
                            row_copy(level, h, i, q).start()

    def scatter_copy(k):
        other, device = near_of(k)
        return pltpu.make_async_remote_copy(
            src_ref=tip_acc.at[pl.ds(other * each, each)],
            dst_ref=tip_near.at[k - 1],
            send_sem=sent.at[2],
            recv_sem=tip_r.at[0],
            device_id=device,
            device_id_type=MESH,
        )

    def far_copy(k):
        return pltpu.make_async_remote_copy(
            src_ref=tip_far.at[place],
            dst_ref=tip_far.at[place],
            send_sem=sent.at[3],
            recv_sem=tip_r.at[1],
            device_id=far_of(k),
            device_id_type=MESH,
        )

    def gather_copy(k):
        mine = pl.ds(seat * each, each)
        return pltpu.make_async_remote_copy(
            src_ref=tip_all.at[mine],
            dst_ref=tip_all.at[mine],
            send_sem=sent.at[4],
            recv_sem=tip_r.at[2],
            device_id=near_of(k)[1],
            device_id_type=MESH,
        )

    def tip_scatter():
        over(near, lambda k: scatter_copy(k).start())

    def tip_reduce():
        all_of(tip_near, tip_r.at[0])
        tip_far[place] = tip_acc[pl.ds(seat * each, each)] + jnp.sum(
            tip_near[...], axis=0
        )
        over(Q, lambda k: far_copy(k).start())

    def tip_total():
        all_of(tip_far.at[pl.ds(1, Q - 1)], tip_r.at[1])
        tip_all[pl.ds(seat * each, each)] = jnp.sum(tip_far[...], axis=0)
        over(near, lambda k: gather_copy(k).start())

    def tip_finish():
        all_of(tip_near, tip_r.at[2])
        tip_rhs_copy.wait()
        for b in range(R // LANES):
            lanes = slice(b * LANES, (b + 1) * LANES)
            total = tip_all[b * groups : (b + 1) * groups].reshape(F, LANES)
            tip_out[:, lanes] = tip_rhs[:, lanes] - total

    def final(h):
        start, n = parts[h]
        out[0, :, start : start + n] = settled(last, h).T

    with scope("rhs"):
        rhs_copy.wait()
        for kind in (1, 2):
            load(0, kind).start()
        cur[0] = rhs_v[...].T
    with scope("split00"):
        split(0, 0)
    tip_c_copy.start()
    tip_rhs_copy.start()
    with scope("barrier"):
        met()
    solve(0, 0)
    pattern_copy.wait()
    for kind in (1, 2):
        with scope("split0"):
            split(0, kind)
    for level in range(1, levels):
        for kind in range(3):
            load(level, kind).start()
    tip_c_copy.wait()

    def splits(level, *kinds):
        for kind in kinds:
            with scope(f"split{level}{kind}"):
                split(level, kind)

    def joins(q, level, h):
        if q < cuts_of(level, h) and not direct(level, h):
            with scope(f"join{level}{h}"):
                join(level, h, q)

    def tips(level, end):
        with scope(f"tip{level}{end}"):
            add_tip(level, 0, end)

    def finals(h):
        with scope(f"final{h}"):
            final(h)

    actions = {
        "P": solve,
        "S": spread,
        "J": functools.partial(joins, 0),
        "K": functools.partial(joins, 1),
        "W": splits,
        "T": tips,
    }
    for step in ORDER:
        actions[step[0]](int(step[1]), int(step[2]))
    with scope("tipreduce"):
        tip_reduce()
    for i in range(2):
        row_copy(last, H - 1, i, 0).start()
    for h in range(H - 2):
        finals(h)
    with scope("tiptotal"):
        tip_total()
    finals(H - 2)
    with scope("tipfinish"):
        tip_finish()
    finals(H - 1)

    with scope("drain"):
        if C > 1:
            all_of(part.at[:, pl.ds(1, C - 1)], sent.at[0])
        all_of(recv, sent.at[1])
        all_of(tip_near, sent.at[2])
        all_of(tip_far.at[pl.ds(1, Q - 1)], sent.at[3])
        all_of(tip_near, sent.at[4])


def solution(mesh):
    T, C = mesh.shape["tm"], mesh.shape["col"]

    def local(rhs, inverse, lower, upper, tile_pattern, tip_coupling, tip_rhs):
        levels, _, block, m = inverse.shape
        R = rhs.shape[2]
        F = tip_rhs.shape[0]
        G = (F // ROWS) * (R // LANES)
        cuts = 2 if m % (2 * LANES) == 0 else 1
        bits = 0
        while bits < 2 and G % (2 ** (bits + 1) * C) == 0 and T % 2 ** (bits + 1) == 0:
            bits += 1
        dims = (levels, T, C, block, m, R, F, tile_pattern.shape[3], bits, cuts)
        H = len(pieces(R))
        tiles_all, tiles_here = tile_pattern.shape[3:]
        Q = T // 2**bits
        f32, b16 = jnp.float32, jnp.bfloat16
        dma = pltpu.SemaphoreType.DMA
        peers = max(C - 1, 1)
        near = 2**bits * C
        anywhere = pl.BlockSpec(memory_space=pl.ANY)
        vmem = pl.BlockSpec(memory_space=pltpu.VMEM)
        return pl.pallas_call(
            functools.partial(kernel, dims),
            out_shape=(
                pltpu.VMEM((1, m, R), f32),
                pltpu.VMEM((F, R), f32),
            ),
            in_specs=[anywhere] * 4
            + [anywhere] * 3,
            out_specs=(vmem, vmem),
            scratch_shapes=[
                pltpu.SMEM((levels, 1, 2, tiles_here, tiles_all), jnp.int32),
                pltpu.VMEM((m, R), f32),
                pltpu.VMEM((levels, 1, F, m), f32),
                pltpu.VMEM((F, R), f32),
                pltpu.VMEM((levels, 3, block, m), f32),
                pltpu.VMEM((levels, 3, block, m), b16),
                pltpu.VMEM((levels, 3, block, m), b16),
                pltpu.VMEM((levels, R, m), f32),
                pltpu.VMEM((levels, C, R, block), f32),
                pltpu.VMEM((levels, R, block), b16),
                pltpu.VMEM((levels, R, block), b16),
                pltpu.VMEM((levels, 2, R, m), f32),
                pltpu.VMEM((levels, 2, R, m), f32),
                pltpu.VMEM((max(levels - 1, 1), R, m), f32),
                pltpu.VMEM((G, ROWS, LANES), f32),
                pltpu.VMEM((near - 1, G // near, ROWS, LANES), f32),
                pltpu.VMEM((Q, G // near, ROWS, LANES), f32),
                pltpu.VMEM((G, ROWS, LANES), f32),
                dma((levels, 3)),
                dma((4,)),
                dma((QUARTERS,)),
                dma((levels, H, peers)),
                dma((max(levels - 1, 1), H, cuts)),
                dma((levels, H)),
                dma((3,)),
                dma((5,)),
            ],
            compiler_params=pltpu.CompilerParams(
                collective_id=0, has_side_effects=True, vmem_limit_bytes=63 * 2**20
            ),
        )(
            rhs,
            inverse,
            lower,
            upper,
            jnp.swapaxes(tile_pattern, 3, 4),
            tip_coupling,
            tip_rhs,
        )

    return jax.shard_map(
        local,
        mesh=mesh,
        in_specs=(
            P("tm", "col", None),
            P(None, "tm", None, "col"),
            P(None, "tm", None, "col"),
            P(None, "tm", None, "col"),
            P(None, "tm", None, None, "col"),
            P(None, "tm", None, "col"),
            P(),
        ),
        out_specs=(P("tm", "col", None), P()),
        check_vma=False,
    )
```

time: 65.7 us -> 63.6 us (0.968)
  Pallas kernels: 63.4 us -> 61.2 us
    pallas_call x1, Pallas kernels: 63.4 us -> 61.2 us  [local(): pl.pallas_call(functools.partial(kernel, dims), out_shape=(pltpu.VMEM((1,...]
where the time goes in v2:
time: 63.6 us; the launch traced here: 63.3 us
  Pallas kernels  61.2 us (96%)
  local copies, waits for them, and re-layouts  1.42 us (2%)
  between operations  0.64 us (1%)
    pallas_call x1, Pallas kernels, local(): pl.pallas_call(functools.partial(kernel, dims), out_shape=(pltpu.VMEM((1,...  61.2 us
    unnamed x2, local copies, waits for them, and re-layouts  1.42 us

profile of v2, /device:TPU:0, one launch (start us, length us, event | category | flops | bytes accessed | tf_op | source)
XLA Modules:
  0.0 63.3 jit_solution(425204601999617652)
XLA Ops:
  0.6 61.2 %shard_map.86 = (f32[1,512,256]{2,1,0:T(8,128)S(1)}, f32[64,256]{1,0:T(8,128)S(1)}) custom-call(f32[1,512,256]{2,1,0:T(8,128)} %rhs_hbm.1, f32[3,1,1024,512]{3,2,1,0:T(8,128)} %inv_hbm.1, f32[3,1,1024,512]{3,2,1,0:T(8,128)} %low_hbm.1, f32[3,1,1024,512]{3,2,1,0:T(8,128)} %up_hbm.1, s32[3,1,2,4,8]{4,3,2,1,0:T(4,128)} %bitcast.1, f32[3,1,64,512]{3,2,1,0:T(8,128)} %tip_c_hbm.1, ...), custom_call_target="tpu_custom_call" | custom-call | tf_op jit(solution)/shard_map/pallas_call | solution.py:505
  61.8 0.8 %copy.11 = f32[1,512,256]{2,1,0:T(8,128)} copy(f32[1,512,256]{2,1,0:T(8,128)S(1)} %get-tuple-element.2) | data formatting | bytes 1048576
  62.6 0.6 copy.12

commit v3 on v2

--- a/solution.py
+++ b/solution.py
@@ -41,7 +41,7 @@
     "K10", "P13", "J11", "S13", "P20", "J12", "S20", "P21", "J13", "S21", "T04", "P22",
     "S22", "T14", "P23", "T23", "S23",
 )
-PIECES = 4
+SIXTEENTHS = (4, 8, 12, 16)
 QUARTERS = 4
 PAIRED = (0,)
 DIRECT = ()
@@ -49,7 +49,8 @@
 
 
 def pieces(R):
-    return tuple((R * h // PIECES, R // PIECES) for h in range(PIECES))
+    ends = [R * e // SIXTEENTHS[-1] for e in SIXTEENTHS]
+    return tuple((a, b - a) for a, b in zip([0] + ends, ends))
 
 
 def kernel(
@@ -242,9 +243,9 @@
         at = (rows_of(h), span(level, h, q))
         arrival = row_r.at[level, h]
         if direct(level, h):
-            target = lax.rem(row + (T - stride if way == 0 else stride), T)
+            target = lax.rem(row + T - stride + 2 * stride * way, T)
             source = send.at[(level, way, *at)]
-        elif way == 0:
+        elif isinstance(way, int) and way == 0:
             target = lax.rem(row + T - 2 * stride + 4 * stride * bit_of(level), T)
             source = send.at[(level, bit_of(level), *at)]
             arrival = join_r.at[level, h, q]
@@ -329,7 +330,8 @@
             s_high[level, rows] = high
             s_low[level, rows] = low
         straight = direct(level, members[0])
-        ways = (0, 1) if straight else (bit_of(level), 1 - bit_of(level))
+        over_end = (row + 2**level) // T
+        ways = (over_end, 1 - over_end) if straight else (bit_of(level), 1 - bit_of(level))
         if closing:
             with scope(f"tip{level}{g}"):
                 add_tip(level, members[0], H)
@@ -348,7 +350,7 @@
                 if not closing and (i == 0 or straight):
                     for h in members:
                         for q in range(cuts_of(level, h)):
-                            row_copy(level, h, i, q).start()
+                            row_copy(level, h, ways[i] if straight else i, q).start()
 
     def scatter_copy(k):
         other, device = near_of(k)
@@ -460,8 +462,9 @@
         actions[step[0]](int(step[1]), int(step[2]))
     with scope("tipreduce"):
         tip_reduce()
-    for i in range(2):
-        row_copy(last, H - 1, i, 0).start()
+    over_end = (row + 2**last) // T
+    for way in (over_end, 1 - over_end):
+        row_copy(last, H - 1, way, 0).start()
     for h in range(H - 2):
         finals(h)
     with scope("tiptotal"):
@@ -478,6 +481,17 @@
         all_of(tip_near, sent.at[2])
         all_of(tip_far.at[pl.ds(1, Q - 1)], sent.at[3])
         all_of(tip_near, sent.at[4])
+
+
+def store(main, tip, main_out, tip_out, sem):
+    copies = [
+        pltpu.make_async_copy(main, main_out, sem.at[0]),
+        pltpu.make_async_copy(tip, tip_out, sem.at[1]),
+    ]
+    for copy in copies:
+        copy.start()
+    for copy in copies:
+        copy.wait()
 
 
 def solution(mesh):
@@ -502,7 +516,7 @@
         near = 2**bits * C
         anywhere = pl.BlockSpec(memory_space=pl.ANY)
         vmem = pl.BlockSpec(memory_space=pltpu.VMEM)
-        return pl.pallas_call(
+        results = pl.pallas_call(
             functools.partial(kernel, dims),
             out_shape=(
                 pltpu.VMEM((1, m, R), f32),
@@ -551,6 +565,16 @@
             tip_coupling,
             tip_rhs,
         )
+        return pl.pallas_call(
+            store,
+            out_shape=(
+                jax.ShapeDtypeStruct((1, m, R), f32),
+                jax.ShapeDtypeStruct((F, R), f32),
+            ),
+            in_specs=[anywhere, anywhere],
+            out_specs=(anywhere, anywhere),
+            scratch_shapes=[dma((2,))],
+        )(*(pltpu.with_memory_space_constraint(x, pltpu.VMEM) for x in results))
 
     return jax.shard_map(
         local,

time: 63.6 us -> 61.5 us (0.967); the launches traced: 63.3 us -> 60.5 us
  local copies, waits for them, and re-layouts: 1.42 us -> 0 us
  Pallas kernels: 61.2 us -> 59.9 us
    pallas_call x1, Pallas kernels: 61.2 us -> 59 us  [local(): pl.pallas_call(functools.partial(kernel, dims), out_shape=(pltpu.VMEM((1,...]
    unnamed x2 -> x0, local copies, waits for them, and re-layouts: 1.42 us -> none
    pallas_call x0 -> x1, Pallas kernels: none -> 0.82 us  [local(): pl.pallas_call(store, out_shape=(jax.ShapeDtypeStruct((1, m, R), f32), ja...]
where the time goes in v3:
time: 61.5 us; the launch traced here: 60.5 us
  Pallas kernels  59.9 us (97%)
  between operations  0.64 us (1%)
    pallas_call x1, Pallas kernels, local(): pl.pallas_call(functools.partial(kernel, dims), out_shape=(pltpu.VMEM((1,...  59 us

profile of v3, /device:TPU:0, one launch (start us, length us, event | category | flops | bytes accessed | tf_op | source)
XLA Modules:
  0.0 60.5 jit_solution(8628163553124220350)
XLA Ops:
  0.6 59.0 %shard_map.86 = (f32[1,512,256]{2,1,0:T(8,128)S(1)}, f32[64,256]{1,0:T(8,128)S(1)}) custom-call(f32[1,512,256]{2,1,0:T(8,128)} %rhs_hbm.1, f32[3,1,1024,512]{3,2,1,0:T(8,128)} %inv_hbm.1, f32[3,1,1024,512]{3,2,1,0:T(8,128)} %low_hbm.1, f32[3,1,1024,512]{3,2,1,0:T(8,128)} %up_hbm.1, s32[3,1,2,4,8]{4,3,2,1,0:T(4,128)} %bitcast.1, f32[3,1,64,512]{3,2,1,0:T(8,128)} %tip_c_hbm.1, ...), custom_call_target="tpu_custom_call" | custom-call | tf_op jit(solution)/shard_map/pallas_call | solution.py:519
  59.7 0.8 %shard_map.87 = (f32[1,512,256]{2,1,0:T(8,128)}, f32[64,256]{1,0:T(8,128)}) custom-call(f32[1,512,256]{2,1,0:T(8,128)S(1)} %get-tuple-element.4.main, f32[64,256]{1,0:T(8,128)S(1)} %get-tuple-element.5.tip), custom_call_target="tpu_custom_call" | custom-call | tf_op jit(solution)/shard_map/pallas_call | solution.py:568

commit v4 on v3

--- a/solution.py
+++ b/solution.py
@@ -160,13 +160,14 @@
                 greet({"tm": other // C, "col": lax.rem(other, C)})
 
             return over(N, anyone)
-        over(near, lambda k: greet(near_of(k)[1]))
-        over(Q, lambda k: greet(far_of(k)))
         greet({"tm": lax.rem(row + T - 2 + 4 * bit_of(1), T), "col": col})
 
         @pl.when(bit_of(0) == bit_of(1))
         def _():
             greet({"tm": lax.rem(row + T - 1 + 2 * bit_of(1), T), "col": col})
+
+        over(Q, lambda k: greet(far_of(k)))
+        over(near, lambda k: greet(near_of(k)[1]))
 
     def met():
         if not by_fours:
@@ -289,8 +290,11 @@
             part[level, 0, rows] = product(
                 stacked, high, w_high[level, 0], w_low[level, 0], NT
             )
-            for k in range(1, C):
-                part_copy(level, g, k).start()
+        if level == 0 and g == 0:
+            with scope("barrier"):
+                met()
+        for k in range(1, C):
+            part_copy(level, g, k).start()
 
     def add_tip(level, first, end):
         start = parts[first][0]
@@ -420,8 +424,6 @@
         split(0, 0)
     tip_c_copy.start()
     tip_rhs_copy.start()
-    with scope("barrier"):
-        met()
     solve(0, 0)
     pattern_copy.wait()
     for kind in (1, 2):

time: 61.5 us -> 60.6 us (0.985); the launches traced: 60.5 us -> 60.4 us
  no operation moved by 1% of the time
where the time goes in v4:
time: 60.6 us; the launch traced here: 60.4 us
  Pallas kernels  59.8 us (99%)
  between operations  0.64 us (1%)
    pallas_call x1, Pallas kernels, local(): pl.pallas_call(functools.partial(kernel, dims), out_shape=(pltpu.VMEM((1,...  59 us

profile of v4, /device:TPU:0, one launch (start us, length us, event | category | flops | bytes accessed | tf_op | source)
XLA Modules:
  0.0 60.4 jit_solution(11946294615018895082)
XLA Ops:
  0.6 59.0 %shard_map.86 = (f32[1,512,256]{2,1,0:T(8,128)S(1)}, f32[64,256]{1,0:T(8,128)S(1)}) custom-call(f32[1,512,256]{2,1,0:T(8,128)} %rhs_hbm.1, f32[3,1,1024,512]{3,2,1,0:T(8,128)} %inv_hbm.1, f32[3,1,1024,512]{3,2,1,0:T(8,128)} %low_hbm.1, f32[3,1,1024,512]{3,2,1,0:T(8,128)} %up_hbm.1, s32[3,1,2,4,8]{4,3,2,1,0:T(4,128)} %bitcast.1, f32[3,1,64,512]{3,2,1,0:T(8,128)} %tip_c_hbm.1, ...), custom_call_target="tpu_custom_call" | custom-call | tf_op jit(solution)/shard_map/pallas_call | solution.py:521
  59.6 0.8 %shard_map.87 = (f32[1,512,256]{2,1,0:T(8,128)}, f32[64,256]{1,0:T(8,128)}) custom-call(f32[1,512,256]{2,1,0:T(8,128)S(1)} %get-tuple-element.4.main, f32[64,256]{1,0:T(8,128)S(1)} %get-tuple-element.5.tip), custom_call_target="tpu_custom_call" | custom-call | tf_op jit(solution)/shard_map/pallas_call | solution.py:570

commit v5 on v4

--- a/solution.py
+++ b/solution.py
@@ -37,15 +37,15 @@
 
 ORDER = (
     "S00", "P01", "W10", "W11", "J00", "S01", "K00", "W12", "W20", "J01", "W21", "W22",
-    "K01", "J02", "P10", "K02", "S10", "J03", "P11", "K03", "S11", "P12", "J10", "S12",
-    "K10", "P13", "J11", "S13", "P20", "J12", "S20", "P21", "J13", "S21", "T04", "P22",
-    "S22", "T14", "P23", "T23", "S23",
+    "K01", "J02", "P10", "K02", "S10", "P11", "J03", "S11", "K03", "P12", "J10", "S12",
+    "K10", "P13", "J11", "S13", "K11", "P20", "J12", "S20", "K12", "P21", "J13", "S21",
+    "K13", "T04", "P22", "S22", "T14", "P23", "T23", "S23",
 )
 SIXTEENTHS = (4, 8, 12, 16)
 QUARTERS = 4
 PAIRED = (0,)
 DIRECT = ()
-HALVED = ((0, 0), (0, 1), (0, 2), (0, 3), (1, 0))
+HALVED = tuple((level, piece) for level in (0, 1) for piece in range(4))
 
 
 def pieces(R):

time: 60.6 us -> 60.8 us (level)
  no operation moved by 1% of the time
where the time goes in v5:
time: 60.8 us; the launch traced here: 60.6 us
  Pallas kernels  60 us (99%)
  between operations  0.64 us (1%)
    pallas_call x1, Pallas kernels, local(): pl.pallas_call(functools.partial(kernel, dims), out_shape=(pltpu.VMEM((1,...  59.2 us

profile of v5, /device:TPU:0, one launch (start us, length us, event | category | flops | bytes accessed | tf_op | source)
XLA Modules:
  0.0 60.6 jit_solution(2563968150365159835)
XLA Ops:
  0.6 59.2 %shard_map.86 = (f32[1,512,256]{2,1,0:T(8,128)S(1)}, f32[64,256]{1,0:T(8,128)S(1)}) custom-call(f32[1,512,256]{2,1,0:T(8,128)} %rhs_hbm.1, f32[3,1,1024,512]{3,2,1,0:T(8,128)} %inv_hbm.1, f32[3,1,1024,512]{3,2,1,0:T(8,128)} %low_hbm.1, f32[3,1,1024,512]{3,2,1,0:T(8,128)} %up_hbm.1, s32[3,1,2,4,8]{4,3,2,1,0:T(4,128)} %bitcast.1, f32[3,1,64,512]{3,2,1,0:T(8,128)} %tip_c_hbm.1, ...), custom_call_target="tpu_custom_call" | custom-call | tf_op jit(solution)/shard_map/pallas_call | solution.py:521
  59.8 0.8 %shard_map.87 = (f32[1,512,256]{2,1,0:T(8,128)}, f32[64,256]{1,0:T(8,128)}) custom-call(f32[1,512,256]{2,1,0:T(8,128)S(1)} %get-tuple-element.4.main, f32[64,256]{1,0:T(8,128)S(1)} %get-tuple-element.5.tip), custom_call_target="tpu_custom_call" | custom-call | tf_op jit(solution)/shard_map/pallas_call | solution.py:570
